TPU v7x, 256 devices: a whole 4x4x8 slice. The times are simulated.
256 devices in a mesh: sub: 32 (over z, x), agg: 8 (over y, core).
Axes of the slice: x: 4, y: 4, z: 8, core: 2. Of those that a mesh axis runs over, the one named last changes fastest.
Arguments:
- dual_load: float32 [8, 32, 64, 1536], P('agg', 'sub'), may hold values from -58 to 58
- interface_inverse: bfloat16 [8, 32, 1536, 1536], P('agg', 'sub'), may hold values from -1 to 2.5, as said below
- dirichlet: bfloat16 [8, 32, 1536, 1536], P('agg', 'sub'), may hold values from -1 to 2.5, as said below
- coupling: bfloat16 [8, 32, 128, 1536], P('agg', 'sub'), may hold values from -0.15625 to 0.15625
- neighbours: int32 [8, 32, 8], P('agg', 'sub'), may hold values from -1 to 31, as said below
- face_counts: int32 [8, 32, 8], P('agg', 'sub'), may hold values from 0 to 192, as said below
- owners: int32 [8, 32, 128, 1], P('agg', 'sub'), may hold values from 0 to 7; in each aligned block of 128 rows (0 to 127, 128 to 255, ..., all dimensions but the last counted through in order) at most 48 rows name the same one
- primal_rows: int32 [8, 32, 128], P('agg', 'sub'), may hold values from 0 to 1023
- coarse_inverse: float32 [8, 1024, 1024], P('agg', 'sub'), may hold values from -1 to 1.5, as said below
Outputs:
- solution: float32 [8, 32, 64, 1536], P('agg', 'sub')
- residual: float32 [8, 32, 64, 1536], P('agg', 'sub')
Inputs may be any that keep to these rules, and one draw needn't show every extreme that they name: `neighbours`: each subdomain lists peers of its own aggregate by their index along sub, -1 in empty slots; no peer twice; if j lists i then i lists j; every listed peer lies within a cyclic distance of 4 along sub. `face_counts`: 0 exactly in empty slots, 48 or more elsewhere; both sides of a face give the same count and hold its rows in the same order. `owners`: among the 128 primal rows of one subdomain no aggregate is named more than 48 times. `interface_inverse`: each subdomain's matrix is symmetric positive definite. `dirichlet`: each subdomain's matrix is symmetric positive definite. `coarse_inverse`: each aggregate's matrix is symmetric positive definite.
All inputs are finite; a program needn't handle non-finite values.
Results may differ from a plain program's by a relative error of at most 0.011.
Values sent between devices are 32-bit elements; how exact they have to be, the bound alone decides.
No kernel may reach another device: no remote copies, remote signals or barrier semaphores. Data moves between devices by JAX's collectives and lax.ppermute only.
A program may use at most 128 MiB of HBM per device.

v0:
```python
import jax
import jax.numpy as jnp
from jax import lax
from jax.sharding import PartitionSpec as P

NC = 1024
CAP = 48
ITERS = 2
FULL_PRECISION = lax.Precision.HIGHEST
CONTRACT_LAST = (((1,), (1,)), ((), ()))


def from_behind_2(block, axis, distance):
    devices = range(lax.axis_size(axis))
    route = [((i - distance) % len(devices), i) for i in devices]
    return lax.ppermute(block, axis, route)


def shards(
    dual_load,
    interface_inverse,
    dirichlet,
    coupling,
    neighbours,
    face_counts,
    owners,
    primal_rows,
    coarse_inverse,
):
    inverse_block = interface_inverse[0, 0]
    dirichlet_block = dirichlet[0, 0]
    coupling_block = coupling[0, 0]
    peer_list = neighbours[0, 0]
    count_list = face_counts[0, 0]
    sub_count = lax.axis_size("sub")
    agg_count = lax.axis_size("agg")
    position = lax.axis_index("sub")
    slot_count = peer_list.shape[0]
    inner_order = inverse_block.shape[0]
    face_depth = inner_order // slot_count
    reach = min(4, (sub_count - 1) // 2)
    inside = (
        (jnp.arange(face_depth, dtype=jnp.int32)[None, :] < count_list[:, None])
        .reshape(1, inner_order)
        .astype(jnp.float32)
    )

    def assemble(local):
        case_count = local.shape[0]
        faces = local.reshape(case_count, slot_count, face_depth)
        placed = jnp.zeros_like(faces)
        for distance in range(1, reach + 1):
            ahead = (position + distance) % sub_count
            behind = (position + sub_count - distance) % sub_count
            to_ahead = (peer_list == ahead).astype(jnp.float32)[None, :, None]
            to_behind = (peer_list == behind).astype(jnp.float32)[None, :, None]
            upward = jnp.sum(faces * to_ahead, axis=1)
            downward = jnp.sum(faces * to_behind, axis=1)
            from_behind = from_behind_2(upward, "sub", distance)
            from_ahead = from_behind_2(downward, "sub", -distance)
            placed = (
                placed + to_behind * from_behind[:, None, :] + to_ahead * from_ahead[:, None, :]
            )
        return inside * (local + placed.reshape(case_count, inner_order))

    owner_ids = owners[0, 0, :, 0]
    row_ids = primal_rows[0, 0]
    owner_hot = (owner_ids[:, None] == jnp.arange(agg_count, dtype=jnp.int32)[None, :]).astype(
        jnp.int32
    )
    earlier = jnp.cumsum(owner_hot, axis=0) - owner_hot
    owner_rank = jnp.sum(earlier * owner_hot, axis=1)
    slot_index = owner_ids * CAP + owner_rank
    packing = slot_index[:, None] == jnp.arange(agg_count * CAP, dtype=jnp.int32)[None, :]
    packing_float = packing.astype(jnp.float32)
    sent_rows = jnp.sum(packing.astype(jnp.int32) * (row_ids[:, None] + 1), axis=0) - 1
    got_rows = lax.all_to_all(sent_rows, "agg", split_axis=0, concat_axis=0, tiled=True)
    scatter_hot = (got_rows[:, None] == jnp.arange(NC, dtype=jnp.int32)[None, :]).astype(
        jnp.float32
    )
    inverse_rows = coarse_inverse[0]

    def precondition(field):
        packed = field.astype(jnp.bfloat16)
        return assemble(
            inside * jnp.dot(packed, dirichlet_block, preferred_element_type=jnp.float32)
        )

    def residual_norm(first, second):
        return lax.psum(jnp.sum(first * second, axis=1), ("sub", "agg"))

    rhs = assemble(inside * dual_load[0, 0])
    solution = jnp.zeros_like(rhs)
    residual = rhs
    precond = precondition(residual)
    direction = precond
    residual_dot = residual_norm(residual, precond)
    for iteration in range(ITERS):
        operator_packed = direction.astype(jnp.bfloat16)
        own = jnp.dot(operator_packed, inverse_block, preferred_element_type=jnp.float32)
        terms = lax.dot_general(
            operator_packed, coupling_block, CONTRACT_LAST, preferred_element_type=jnp.float32
        )
        outgoing = jnp.dot(terms, packing_float, precision=FULL_PRECISION)
        gathered = jnp.dot(
            lax.all_to_all(outgoing, "agg", split_axis=1, concat_axis=1, tiled=True),
            scatter_hot,
            precision=FULL_PRECISION,
        )
        coarse_rhs = lax.psum(gathered, "sub")
        partial_rows = lax.dot_general(
            coarse_rhs, inverse_rows, CONTRACT_LAST, precision=FULL_PRECISION
        )
        coarse_sol = lax.all_gather(partial_rows, "sub", axis=1, tiled=True)
        answer = lax.dot_general(coarse_sol, scatter_hot, CONTRACT_LAST, precision=FULL_PRECISION)
        returned = lax.all_to_all(answer, "agg", split_axis=1, concat_axis=1, tiled=True)
        local_back = lax.dot_general(
            returned, packing_float, CONTRACT_LAST, precision=FULL_PRECISION
        )
        correction = jnp.dot(
            local_back.astype(jnp.bfloat16), coupling_block, preferred_element_type=jnp.float32
        )
        image = assemble(inside * (own + correction))
        alpha = (residual_dot / lax.psum(jnp.sum(direction * image, axis=1), ("sub", "agg")))[
            :, None
        ]
        solution = solution + alpha * direction
        residual = residual - alpha * image
        if iteration + 1 < ITERS:
            precond = precondition(residual)
            next_dot = residual_norm(residual, precond)
            direction = precond + (next_dot / residual_dot)[:, None] * direction
            residual_dot = next_dot
    return (solution[None, None], residual[None, None])


def solution(mesh):
    in_specs = (
        P("agg", "sub", None, None),
        P("agg", "sub", None, None),
        P("agg", "sub", None, None),
        P("agg", "sub", None, None),
        P("agg", "sub", None),
        P("agg", "sub", None),
        P("agg", "sub", None, None),
        P("agg", "sub", None),
        P("agg", "sub", None),
    )
    out_specs = (P("agg", "sub", None, None), P("agg", "sub", None, None))
    return jax.shard_map(shards, mesh=mesh, in_specs=in_specs, out_specs=out_specs, check_vma=False)
```

profile of v0, /device:TPU:1, one launch (start us, length us, event | category | flops | bytes accessed | tf_op | source)
XLA Modules:
  0.0 917.8 jit_solution(6425770265424465426)
XLA Ops:
  13.6 6.6 collective-permute-start.1
  20.4 2.7 collective-permute-start.7
  28.4 2.6 collective-permute-start.3
  50.8 5.2 fusion.8
  58.0 2.5 multiply_reduce_fusion.31
  60.5 4.7 collective-permute-start.11
  65.2 2.7 collective-permute-start.9
  76.5 10.1 %all-to-all-start.1 = ((s32[8,48,1]{1,2,0:T(1,128)}), s32[8,48,1]{1,2,0:T(1,128)}, u32[]{:S(2)}, u32[]{:S(2)}) async-start(s32[8,48,1]{1,2,0:T(1,128)} %bitcast.111), calls=%async_computation.1 | async-start | bytes 8192 | tf_op jit(solution)/shard_map/all_to_all | solution.py:77
  119.4 4.8 all-to-all-start
  136.4 138.3 %all-reduce.4.cloned.1.call-done = f32[64,1024]{1,0:T(8,128)} async-done(((f32[64,1024]{1,0:T(8,128)}), f32[64,1024]{1,0:T(8,128)}) %all-reduce.4.cloned.1.call-update) | async-done | bytes 262160 | tf_op jit(solution)/shard_map/psum | solution.py:110
  275.9 35.9 %all_gather.6 = f32[64,1024]{0,1:T(8,128)S(1)} all-gather(f32[64,32]{0,1:T(8,128)S(1)} %fusion.58), channel_id=1, replica_groups=mesh['sub'=32,'agg'=8] {'sub'}, dimensions={1}, use_global_device_ids=true | all-gather | bytes 270336 | tf_op jit(solution)/shard_map/all_gather | solution.py:114
  315.8 26.7 %all_to_all.54 = f32[8,1,3072]{2,1,0:T(1,128)} all-to-all(f32[8,1,3072]{2,1,0:T(1,128)} %reshape.670), channel_id=1, replica_groups=mesh['sub'=32,'agg'=8] {'agg'}, dimensions={0} | all-to-all | bytes 196608 | tf_op jit(solution)/shard_map/all_to_all | solution.py:116
  348.1 4.0 fusion.23
  354.1 3.2 multiply_reduce_fusion.23
  360.2 4.5 collective-permute-start.17
  364.7 3.8 collective-permute-start.21
  368.5 2.7 collective-permute-start.23
  394.4 3.9 multiply_reduce_fusion.42
  398.5 77.6 %all-reduce = (f32[64]{0:T(128)S(1)}, f32[64]{0:T(128)S(1)}) all-reduce(f32[64]{0:T(128)S(1)} %get-tuple-element.43, f32[64]{0:T(128)S(1)} %get-tuple-element.42), channel_id=1, replica_groups=mesh['sub'=32,'agg'=8] {'sub','agg'}, use_global_device_ids=true, to_apply=%region_17.18 | all-reduce | flops 128 | bytes 1024 | tf_op jit(solution)/shard_map/psum | solution.py:90
  477.2 3.3 fusion.11
  488.2 3.5 collective-permute-start.29
  491.7 2.7 collective-permute-start.31
  505.9 77.6 %psum.45 = f32[64]{0:T(128)S(1)} all-reduce(f32[64]{0:T(128)S(1)} %get-tuple-element.48), channel_id=1, replica_groups=mesh['sub'=32,'agg'=8] {'sub','agg'}, use_global_device_ids=true, to_apply=%region_41.42 | all-reduce | flops 64 | bytes 512 | tf_op jit(solution)/shard_map/psum | solution.py:90
  585.7 8.1 all_to_all.55
  596.3 136.3 %all-reduce.6.cloned.1.call-done = f32[64,1024]{1,0:T(8,128)} async-done(((f32[64,1024]{1,0:T(8,128)}), f32[64,1024]{1,0:T(8,128)}) %all-reduce.6.cloned.1.call-update) | async-done | bytes 262160 | tf_op jit(solution)/shard_map/psum | solution.py:110
  733.9 35.9 %all_gather.7 = f32[64,1024]{0,1:T(8,128)S(1)} all-gather(f32[64,32]{0,1:T(8,128)S(1)} %fusion.56), channel_id=1, replica_groups=mesh['sub'=32,'agg'=8] {'sub'}, dimensions={1}, use_global_device_ids=true | all-gather | bytes 270336 | tf_op jit(solution)/shard_map/all_gather | solution.py:114
  770.8 26.7 %all_to_all.56 = f32[8,1,3072]{2,1,0:T(1,128)S(1)} all-to-all(f32[8,1,3072]{2,1,0:T(1,128)S(1)} %reshape.674), channel_id=1, replica_groups=mesh['sub'=32,'agg'=8] {'agg'}, dimensions={0} | all-to-all | bytes 196608 | tf_op jit(solution)/shard_map/all_to_all | solution.py:116
  799.1 3.3 fusion.20
  807.2 4.5 collective-permute-start.33
  811.7 3.6 collective-permute-start.37
  815.3 2.7 collective-permute-start.39
  831.3 77.7 %psum.47 = f32[64]{0:T(128)S(1)} all-reduce(f32[64]{0:T(128)S(1)} %get-tuple-element.46), channel_id=1, replica_groups=mesh['sub'=32,'agg'=8] {'sub','agg'}, use_global_device_ids=true, to_apply=%region_52.53 | all-reduce | flops 64 | bytes 512 | tf_op jit(solution)/shard_map/psum | solution.py:124
  (347 shorter events, 174.0 us)
Async XLA Ops:
  11.5 35.6 %collective-permute-start = (f32[64,192]{1,0:T(8,128)S(1)}, f32[64,192]{1,0:T(8,128)}, u32[]{:S(2)}, u32[]{:S(2)}) collective-permute-start(f32[64,192]{1,0:T(8,128)S(1)} %get-tuple-element.2), channel_id=1, source_target_pairs={{248,0},{0,8},{8,16},{16,24},{24,32},{32,40},{40,48},{48,56},{56,6... | collective-permute-start | bytes 147464 | tf_op jit(solution)/shard_map/ppermute | solution.py:16
  13.6 29.9 %collective-permute-start.1 = (f32[64,192]{1,0:T(8,128)}, f32[64,192]{1,0:T(8,128)}, u32[]{:S(2)}, u32[]{:S(2)}) collective-permute-start(f32[64,192]{1,0:T(8,128)} %get-tuple-element.3), channel_id=1, source_target_pairs={{8,0},{16,8},{24,16},{32,24},{40,32},{48,40},{56,48},{64,56},{72,6... | collective-permute-start | bytes 147464 | tf_op jit(solution)/shard_map/ppermute | solution.py:16
  20.4 10.7 %collective-permute-start.7 = (f32[64,192]{1,0:T(8,128)S(1)}, f32[64,192]{1,0:T(8,128)S(1)}, u32[]{:S(2)}, u32[]{:S(2)}) collective-permute-start(f32[64,192]{1,0:T(8,128)S(1)} %get-tuple-element.9), channel_id=1, source_target_pairs={{32,0},{40,8},{48,16},{56,24},{64,32},{72,40},{80,48},{88,56},{96,... | collective-permute-start | bytes 147464 | tf_op jit(solution)/shard_map/ppermute | solution.py:16
  26.0 13.9 %collective-permute-start.2 = (f32[64,192]{1,0:T(8,128)}, f32[64,192]{1,0:T(8,128)}, u32[]{:S(2)}, u32[]{:S(2)}) collective-permute-start(f32[64,192]{1,0:T(8,128)} %get-tuple-element.4), channel_id=1, source_target_pairs={{240,0},{248,8},{0,16},{8,24},{16,32},{24,40},{32,48},{40,56},{48,... | collective-permute-start | bytes 147464 | tf_op jit(solution)/shard_map/ppermute | solution.py:16
  28.4 9.6 %collective-permute-start.3 = (f32[64,192]{1,0:T(8,128)S(1)}, f32[64,192]{1,0:T(8,128)}, u32[]{:S(2)}, u32[]{:S(2)}) collective-permute-start(f32[64,192]{1,0:T(8,128)S(1)} %get-tuple-element.5), channel_id=1, source_target_pairs={{16,0},{24,8},{32,16},{40,24},{48,32},{56,40},{64,48},{72,56},{80,... | collective-permute-start | bytes 147464 | tf_op jit(solution)/shard_map/ppermute | solution.py:16
  68.6 41.9 %collective-permute-start.8 = (f32[64,192]{1,0:T(8,128)S(1)}, f32[64,192]{1,0:T(8,128)S(1)}, u32[]{:S(2)}, u32[]{:S(2)}) collective-permute-start(f32[64,192]{1,0:T(8,128)S(1)} %get-tuple-element.34), channel_id=1, source_target_pairs={{248,0},{0,8},{8,16},{16,24},{24,32},{32,40},{40,48},{48,56},{56,6... | collective-permute-start | bytes 147464 | tf_op jit(solution)/shard_map/ppermute | solution.py:16
  68.7 39.0 %collective-permute-start.15 = (f32[64,192]{1,0:T(8,128)S(1)}, f32[64,192]{1,0:T(8,128)S(1)}, u32[]{:S(2)}, u32[]{:S(2)}) collective-permute-start(f32[64,192]{1,0:T(8,128)S(1)} %get-tuple-element.35), channel_id=1, source_target_pairs={{32,0},{40,8},{48,16},{56,24},{64,32},{72,40},{80,48},{88,56},{96,... | collective-permute-start | bytes 147464 | tf_op jit(solution)/shard_map/ppermute | solution.py:16
  68.8 35.2 %collective-permute-start.14 = (f32[64,192]{1,0:T(8,128)S(1)}, f32[64,192]{1,0:T(8,128)}, u32[]{:S(2)}, u32[]{:S(2)}) collective-permute-start(f32[64,192]{1,0:T(8,128)S(1)} %get-tuple-element.36), channel_id=1, source_target_pairs={{224,0},{232,8},{240,16},{248,24},{0,32},{8,40},{16,48},{24,56},{3... | collective-permute-start | bytes 147464 | tf_op jit(solution)/shard_map/ppermute | solution.py:16
  71.9 28.5 %collective-permute-start.13 = (f32[64,192]{1,0:T(8,128)S(1)}, f32[64,192]{1,0:T(8,128)}, u32[]{:S(2)}, u32[]{:S(2)}) collective-permute-start(f32[64,192]{1,0:T(8,128)S(1)} %get-tuple-element.37), channel_id=1, source_target_pairs={{24,0},{32,8},{40,16},{48,24},{56,32},{64,40},{72,48},{80,56},{88,... | collective-permute-start | bytes 147464 | tf_op jit(solution)/shard_map/ppermute | solution.py:16
  73.5 23.3 %collective-permute-start.12 = (f32[64,192]{1,0:T(8,128)S(1)}, f32[64,192]{1,0:T(8,128)}, u32[]{:S(2)}, u32[]{:S(2)}) collective-permute-start(f32[64,192]{1,0:T(8,128)S(1)} %get-tuple-element.38), channel_id=1, source_target_pairs={{232,0},{240,8},{248,16},{0,24},{8,32},{16,40},{24,48},{32,56},{40... | collective-permute-start | bytes 147464 | tf_op jit(solution)/shard_map/ppermute | solution.py:16
  76.5 42.9 %all-to-all-start.1 = ((s32[8,48,1]{1,2,0:T(1,128)}), s32[8,48,1]{1,2,0:T(1,128)}, u32[]{:S(2)}, u32[]{:S(2)}) async-start(s32[8,48,1]{1,2,0:T(1,128)} %bitcast.111), calls=%async_computation.1 | async-start | bytes 8192 | tf_op jit(solution)/shard_map/all_to_all | solution.py:77
  119.4 9.9 %all-to-all-start = ((f32[8,1,3072]{2,1,0:T(1,128)}), f32[8,1,3072]{2,1,0:T(1,128)}, u32[]{:S(2)}, u32[]{:S(2)}) async-start(f32[8,1,3072]{2,1,0:T(1,128)} %reshape.668), calls=%async_computation | async-start | bytes 196608 | tf_op jit(solution)/shard_map/all_to_all | solution.py:106
  124.2 150.4 %all-reduce.4.cloned.1.call-start = ((), (), s32[]{:S(2)}) async-start(), calls=%async_computation.5 | async-start | bytes 524288 | tf_op jit(solution)/shard_map/psum | solution.py:110
  136.3 596.3 %all-reduce.6.cloned.1.call-start = ((), (), s32[]{:S(2)}) async-start(), calls=%async_computation.6 | async-start | bytes 524288 | tf_op jit(solution)/shard_map/psum | solution.py:110
  357.3 11.3 %collective-permute-start.19 = (f32[64,192]{1,0:T(8,128)S(1)}, f32[64,192]{1,0:T(8,128)}, u32[]{:S(2)}, u32[]{:S(2)}) collective-permute-start(f32[64,192]{1,0:T(8,128)S(1)} %get-tuple-element.31), channel_id=1, source_target_pairs={{16,0},{24,8},{32,16},{40,24},{48,32},{56,40},{64,48},{72,56},{80,... | collective-permute-start | bytes 147464 | tf_op jit(solution)/shard_map/ppermute | solution.py:16
  359.2 9.3 %collective-permute-start.18 = (f32[64,192]{1,0:T(8,128)S(1)}, f32[64,192]{1,0:T(8,128)}, u32[]{:S(2)}, u32[]{:S(2)}) collective-permute-start(f32[64,192]{1,0:T(8,128)S(1)} %get-tuple-element.32), channel_id=1, source_target_pairs={{240,0},{248,8},{0,16},{8,24},{16,32},{24,40},{32,48},{40,56},{48,... | collective-permute-start | bytes 147464 | tf_op jit(solution)/shard_map/ppermute | solution.py:16
  360.2 11.0 %collective-permute-start.17 = (f32[64,192]{1,0:T(8,128)S(1)}, f32[64,192]{1,0:T(8,128)}, u32[]{:S(2)}, u32[]{:S(2)}) collective-permute-start(f32[64,192]{1,0:T(8,128)S(1)} %get-tuple-element.33), channel_id=1, source_target_pairs={{8,0},{16,8},{24,16},{32,24},{40,32},{48,40},{56,48},{64,56},{72,6... | collective-permute-start | bytes 147464 | tf_op jit(solution)/shard_map/ppermute | solution.py:16
  364.7 20.5 %collective-permute-start.20 = (f32[64,192]{1,0:T(8,128)}, f32[64,192]{1,0:T(8,128)}, u32[]{:S(2)}, u32[]{:S(2)}) collective-permute-start(f32[64,192]{1,0:T(8,128)} %get-tuple-element.30), channel_id=1, source_target_pairs={{232,0},{240,8},{248,16},{0,24},{8,32},{16,40},{24,48},{32,56},{40... | collective-permute-start | bytes 147464 | tf_op jit(solution)/shard_map/ppermute | solution.py:16
  364.7 22.3 %collective-permute-start.21 = (f32[64,192]{1,0:T(8,128)}, f32[64,192]{1,0:T(8,128)}, u32[]{:S(2)}, u32[]{:S(2)}) collective-permute-start(f32[64,192]{1,0:T(8,128)} %get-tuple-element.29), channel_id=1, source_target_pairs={{24,0},{32,8},{40,16},{48,24},{56,32},{64,40},{72,48},{80,56},{88,... | collective-permute-start | bytes 147464 | tf_op jit(solution)/shard_map/ppermute | solution.py:16
  368.5 20.4 %collective-permute-start.22 = (f32[64,192]{1,0:T(8,128)}, f32[64,192]{1,0:T(8,128)}, u32[]{:S(2)}, u32[]{:S(2)}) collective-permute-start(f32[64,192]{1,0:T(8,128)} %get-tuple-element.28), channel_id=1, source_target_pairs={{224,0},{232,8},{240,16},{248,24},{0,32},{8,40},{16,48},{24,56},{3... | collective-permute-start | bytes 147464 | tf_op jit(solution)/shard_map/ppermute | solution.py:16
  368.5 22.2 %collective-permute-start.23 = (f32[64,192]{1,0:T(8,128)}, f32[64,192]{1,0:T(8,128)}, u32[]{:S(2)}, u32[]{:S(2)}) collective-permute-start(f32[64,192]{1,0:T(8,128)} %get-tuple-element.27), channel_id=1, source_target_pairs={{32,0},{40,8},{48,16},{56,24},{64,32},{72,40},{80,48},{88,56},{96,... | collective-permute-start | bytes 147464 | tf_op jit(solution)/shard_map/ppermute | solution.py:16
  371.2 21.3 %collective-permute-start.16 = (f32[64,192]{1,0:T(8,128)}, f32[64,192]{1,0:T(8,128)}, u32[]{:S(2)}, u32[]{:S(2)}) collective-permute-start(f32[64,192]{1,0:T(8,128)} %get-tuple-element.26), channel_id=1, source_target_pairs={{248,0},{0,8},{8,16},{16,24},{24,32},{32,40},{40,48},{48,56},{56,6... | collective-permute-start | bytes 147464 | tf_op jit(solution)/shard_map/ppermute | solution.py:16
  482.7 9.0 collective-permute-start.27
  485.6 8.7 collective-permute-start.25
  488.2 8.7 collective-permute-start.29
  491.7 8.8 collective-permute-start.31
  804.3 11.0 %collective-permute-start.35 = (f32[64,192]{1,0:T(8,128)S(1)}, f32[64,192]{1,0:T(8,128)S(1)}, u32[]{:S(2)}, u32[]{:S(2)}) collective-permute-start(f32[64,192]{1,0:T(8,128)S(1)} %get-tuple-element.15), channel_id=1, source_target_pairs={{16,0},{24,8},{32,16},{40,24},{48,32},{56,40},{64,48},{72,56},{80,... | collective-permute-start | bytes 147464 | tf_op jit(solution)/shard_map/ppermute | solution.py:16
  806.2 9.1 collective-permute-start.34
  807.2 10.8 %collective-permute-start.33 = (f32[64,192]{1,0:T(8,128)S(1)}, f32[64,192]{1,0:T(8,128)S(1)}, u32[]{:S(2)}, u32[]{:S(2)}) collective-permute-start(f32[64,192]{1,0:T(8,128)S(1)} %get-tuple-element.17), channel_id=1, source_target_pairs={{8,0},{16,8},{24,16},{32,24},{40,32},{48,40},{56,48},{64,56},{72,6... | collective-permute-start | bytes 147464 | tf_op jit(solution)/shard_map/ppermute | solution.py:16
  811.7 10.3 %collective-permute-start.37 = (f32[64,192]{1,0:T(8,128)}, f32[64,192]{1,0:T(8,128)}, u32[]{:S(2)}, u32[]{:S(2)}) collective-permute-start(f32[64,192]{1,0:T(8,128)} %get-tuple-element.13), channel_id=1, source_target_pairs={{24,0},{32,8},{40,16},{48,24},{56,32},{64,40},{72,48},{80,56},{88,... | collective-permute-start | bytes 147464 | tf_op jit(solution)/shard_map/ppermute | solution.py:16
  815.3 10.3 %collective-permute-start.39 = (f32[64,192]{1,0:T(8,128)S(1)}, f32[64,192]{1,0:T(8,128)}, u32[]{:S(2)}, u32[]{:S(2)}) collective-permute-start(f32[64,192]{1,0:T(8,128)S(1)} %get-tuple-element.11), channel_id=1, source_target_pairs={{32,0},{40,8},{48,16},{56,24},{64,32},{72,40},{80,48},{88,56},{96,... | collective-permute-start | bytes 147464 | tf_op jit(solution)/shard_map/ppermute | solution.py:16
  818.0 9.5 %collective-permute-start.32 = (f32[64,192]{1,0:T(8,128)S(1)}, f32[64,192]{1,0:T(8,128)}, u32[]{:S(2)}, u32[]{:S(2)}) collective-permute-start(f32[64,192]{1,0:T(8,128)S(1)} %get-tuple-element.10), channel_id=1, source_target_pairs={{248,0},{0,8},{8,16},{16,24},{24,32},{32,40},{40,48},{48,56},{56,6... | collective-permute-start | bytes 147464 | tf_op jit(solution)/shard_map/ppermute | solution.py:16
  (68 other events, 2431.6 us)
Sparse Core Ops, SparseCore 0:
  136.4 138.1 all-reduce.3
  596.4 136.1 all-reduce.5
where the time goes:
time: 927 us; the launch traced here: 918 us
  blocking collectives  366 us (39%)
  waiting for transfers between devices  278 us (30%)
  local copies, waits for them, and re-layouts  105 us (11%)
  starting transfers between devices  83.3 us (9%)
  other arithmetic  39.7 us (4%)
  matrix products  30.5 us (3%)
  between operations  15.6 us (2%)
    psum x2, waiting for transfers between devices, shards(): coarse_rhs = lax.psum(gathered, 'sub')  275 us
    psum x2, blocking collectives, residual_norm(): return lax.psum(jnp.sum(first * second, axis=1), ('sub', 'agg'))  155 us
    psum x1, blocking collectives, shards(): lax.psum(jnp.sum(direction * image, axis=1), ('sub', 'agg'))  77.7 us
    all_gather x2, blocking collectives, shards(): coarse_sol = lax.all_gather(partial_rows, 'sub', axis=1, tiled=True)  71.7 us
    ppermute x40, starting transfers between devices, from_behind_2(): return lax.ppermute(block, axis, route)  68.3 us
    all_to_all x2, blocking collectives, shards(): lax.all_to_all(answer, 'agg', split_axis=1, concat_axis=1, tiled=True)  53.4 us
    mul x52, local copies, waits for them, and re-layouts, assemble(): to_behind * from_behind[:, None, :]  46.7 us
    mul x44, local copies, waits for them, and re-layouts, assemble(): to_ahead * from_ahead[:, None, :]  40.9 us
  transfers between devices with their start and end apart: 44, of which 4 were waited for; matrix products, arithmetic and copies ran while one was open for 10% of the time, Pallas kernels for 0%

commit v1 on v0

--- a/solution.py
+++ b/solution.py
@@ -113,7 +113,10 @@
         )
         coarse_sol = lax.all_gather(partial_rows, "sub", axis=1, tiled=True)
         answer = lax.dot_general(coarse_sol, scatter_hot, CONTRACT_LAST, precision=FULL_PRECISION)
-        returned = lax.all_to_all(answer, "agg", split_axis=1, concat_axis=1, tiled=True)
+        returned = jnp.concatenate(
+            lax.all_to_all(jnp.stack(jnp.split(answer, lax.axis_size("agg"), axis=1)), "agg", 0, 0),
+            axis=1,
+        )
         local_back = lax.dot_general(
             returned, packing_float, CONTRACT_LAST, precision=FULL_PRECISION
         )

time: 927 us -> 935 us (level)
  no operation moved by 1% of the time
where the time goes in v1:
time: 935 us; the launch traced here: 926 us
  blocking collectives  366 us (39%)
  waiting for transfers between devices  278 us (30%)
  local copies, waits for them, and re-layouts  113 us (12%)
  starting transfers between devices  83.3 us (9%)
  other arithmetic  39.7 us (4%)
  matrix products  30.3 us (3%)
  between operations  15.6 us (2%)
    psum x2, waiting for transfers between devices, shards(): coarse_rhs = lax.psum(gathered, 'sub')  275 us
    psum x2, blocking collectives, residual_norm(): return lax.psum(jnp.sum(first * second, axis=1), ('sub', 'agg'))  155 us
    psum x1, blocking collectives, shards(): lax.psum(jnp.sum(direction * image, axis=1), ('sub', 'agg'))  77.7 us
    all_gather x2, blocking collectives, shards(): coarse_sol = lax.all_gather(partial_rows, 'sub', axis=1, tiled=True)  71.7 us
    ppermute x40, starting transfers between devices, from_behind_2(): return lax.ppermute(block, axis, route)  68.3 us
    all_to_all x2, blocking collectives, shards(): lax.all_to_all(jnp.stack(jnp.split(answer, lax.axis_size('agg'), axis=1))...  53.4 us
    mul x52, local copies, waits for them, and re-layouts, assemble(): to_behind * from_behind[:, None, :]  46.7 us
    mul x44, local copies, waits for them, and re-layouts, assemble(): to_ahead * from_ahead[:, None, :]  40.9 us
  transfers between devices with their start and end apart: 44, of which 4 were waited for; matrix products, arithmetic and copies ran while one was open for 10% of the time, Pallas kernels for 0%

profile of v1, /device:TPU:1, one launch (start us, length us, event | category | flops | bytes accessed | tf_op | source)
XLA Modules:
  0.0 925.5 jit_solution(4207860750517160455)
XLA Ops:
  13.6 6.6 collective-permute-start.1
  20.4 2.7 collective-permute-start.7
  28.4 2.6 collective-permute-start.3
  50.8 5.2 fusion.8
  60.5 4.7 collective-permute-start.11
  65.2 2.7 collective-permute-start.9
  76.5 10.1 %all-to-all-start.1 = ((s32[8,48,1]{1,2,0:T(1,128)}), s32[8,48,1]{1,2,0:T(1,128)}, u32[]{:S(2)}, u32[]{:S(2)}) async-start(s32[8,48,1]{1,2,0:T(1,128)} %bitcast.177), calls=%async_computation.1 | async-start | bytes 8192 | tf_op jit(solution)/shard_map/all_to_all | solution.py:77
  119.4 4.8 all-to-all-start
  136.4 138.3 %all-reduce.4.cloned.1.call-done = f32[64,1024]{1,0:T(8,128)} async-done(((f32[64,1024]{1,0:T(8,128)}), f32[64,1024]{1,0:T(8,128)}) %all-reduce.4.cloned.1.call-update) | async-done | bytes 262160 | tf_op jit(solution)/shard_map/psum | solution.py:110
  275.9 35.9 %all_gather.6 = f32[64,1024]{0,1:T(8,128)S(1)} all-gather(f32[64,32]{0,1:T(8,128)S(1)} %fusion.58), channel_id=1, replica_groups=mesh['sub'=32,'agg'=8] {'sub'}, dimensions={1}, use_global_device_ids=true | all-gather | bytes 270336 | tf_op jit(solution)/shard_map/all_gather | solution.py:114
  322.6 26.7 %all_to_all.40 = f32[8,1,3072]{2,1,0:T(1,128)} all-to-all(f32[8,1,3072]{2,1,0:T(1,128)} %reshape.682), channel_id=1, replica_groups=mesh['sub'=32,'agg'=8] {'agg'}, dimensions={0} | all-to-all | bytes 196608 | tf_op jit(solution)/shard_map/all_to_all | solution.py:117
  354.8 4.0 fusion.23
  360.8 3.2 multiply_reduce_fusion.23
  367.0 4.5 collective-permute-start.17
  371.7 3.6 collective-permute-start.21
  375.2 2.7 collective-permute-start.23
  401.1 3.9 multiply_reduce_fusion.42
  405.2 77.6 %all-reduce = (f32[64]{0:T(128)S(1)}, f32[64]{0:T(128)S(1)}) all-reduce(f32[64]{0:T(128)S(1)} %get-tuple-element.43, f32[64]{0:T(128)S(1)} %get-tuple-element.42), channel_id=1, replica_groups=mesh['sub'=32,'agg'=8] {'sub','agg'}, use_global_device_ids=true, to_apply=%region_17.18 | all-reduce | flops 128 | bytes 1024 | tf_op jit(solution)/shard_map/psum | solution.py:90
  483.9 3.3 fusion.11
  492.3 2.6 collective-permute-start.25
  494.9 3.6 collective-permute-start.29
  498.5 2.7 collective-permute-start.31
  512.7 77.6 %psum.45 = f32[64]{0:T(128)S(1)} all-reduce(f32[64]{0:T(128)S(1)} %get-tuple-element.48), channel_id=1, replica_groups=mesh['sub'=32,'agg'=8] {'sub','agg'}, use_global_device_ids=true, to_apply=%region_41.42 | all-reduce | flops 64 | bytes 512 | tf_op jit(solution)/shard_map/psum | solution.py:90
  592.5 8.1 all_to_all.41
  603.1 136.3 %all-reduce.6.cloned.1.call-done = f32[64,1024]{1,0:T(8,128)} async-done(((f32[64,1024]{1,0:T(8,128)}), f32[64,1024]{1,0:T(8,128)}) %all-reduce.6.cloned.1.call-update) | async-done | bytes 262160 | tf_op jit(solution)/shard_map/psum | solution.py:110
  740.6 35.9 %all_gather.7 = f32[64,1024]{0,1:T(8,128)S(1)} all-gather(f32[64,32]{0,1:T(8,128)S(1)} %fusion.56), channel_id=1, replica_groups=mesh['sub'=32,'agg'=8] {'sub'}, dimensions={1}, use_global_device_ids=true | all-gather | bytes 270336 | tf_op jit(solution)/shard_map/all_gather | solution.py:114
  778.5 26.7 %all_to_all.42 = f32[8,1,3072]{2,1,0:T(1,128)S(1)} all-to-all(f32[8,1,3072]{2,1,0:T(1,128)S(1)} %reshape.686), channel_id=1, replica_groups=mesh['sub'=32,'agg'=8] {'agg'}, dimensions={0} | all-to-all | bytes 196608 | tf_op jit(solution)/shard_map/all_to_all | solution.py:117
  806.8 3.3 fusion.20
  814.9 4.5 collective-permute-start.33
  819.4 3.6 collective-permute-start.37
  823.0 2.7 collective-permute-start.39
  839.0 77.7 %psum.47 = f32[64]{0:T(128)S(1)} all-reduce(f32[64]{0:T(128)S(1)} %get-tuple-element.46), channel_id=1, replica_groups=mesh['sub'=32,'agg'=8] {'sub','agg'}, use_global_device_ids=true, to_apply=%region_52.53 | all-reduce | flops 64 | bytes 512 | tf_op jit(solution)/shard_map/psum | solution.py:127
  (365 shorter events, 181.8 us)
Async XLA Ops:
  11.5 35.6 %collective-permute-start = (f32[64,192]{1,0:T(8,128)S(1)}, f32[64,192]{1,0:T(8,128)}, u32[]{:S(2)}, u32[]{:S(2)}) collective-permute-start(f32[64,192]{1,0:T(8,128)S(1)} %get-tuple-element.2), channel_id=1, source_target_pairs={{248,0},{0,8},{8,16},{16,24},{24,32},{32,40},{40,48},{48,56},{56,6... | collective-permute-start | bytes 147464 | tf_op jit(solution)/shard_map/ppermute | solution.py:16
  13.6 29.9 %collective-permute-start.1 = (f32[64,192]{1,0:T(8,128)}, f32[64,192]{1,0:T(8,128)}, u32[]{:S(2)}, u32[]{:S(2)}) collective-permute-start(f32[64,192]{1,0:T(8,128)} %get-tuple-element.3), channel_id=1, source_target_pairs={{8,0},{16,8},{24,16},{32,24},{40,32},{48,40},{56,48},{64,56},{72,6... | collective-permute-start | bytes 147464 | tf_op jit(solution)/shard_map/ppermute | solution.py:16
  20.4 10.7 %collective-permute-start.7 = (f32[64,192]{1,0:T(8,128)S(1)}, f32[64,192]{1,0:T(8,128)S(1)}, u32[]{:S(2)}, u32[]{:S(2)}) collective-permute-start(f32[64,192]{1,0:T(8,128)S(1)} %get-tuple-element.9), channel_id=1, source_target_pairs={{32,0},{40,8},{48,16},{56,24},{64,32},{72,40},{80,48},{88,56},{96,... | collective-permute-start | bytes 147464 | tf_op jit(solution)/shard_map/ppermute | solution.py:16
  26.0 13.9 %collective-permute-start.2 = (f32[64,192]{1,0:T(8,128)}, f32[64,192]{1,0:T(8,128)}, u32[]{:S(2)}, u32[]{:S(2)}) collective-permute-start(f32[64,192]{1,0:T(8,128)} %get-tuple-element.4), channel_id=1, source_target_pairs={{240,0},{248,8},{0,16},{8,24},{16,32},{24,40},{32,48},{40,56},{48,... | collective-permute-start | bytes 147464 | tf_op jit(solution)/shard_map/ppermute | solution.py:16
  28.4 9.6 %collective-permute-start.3 = (f32[64,192]{1,0:T(8,128)S(1)}, f32[64,192]{1,0:T(8,128)}, u32[]{:S(2)}, u32[]{:S(2)}) collective-permute-start(f32[64,192]{1,0:T(8,128)S(1)} %get-tuple-element.5), channel_id=1, source_target_pairs={{16,0},{24,8},{32,16},{40,24},{48,32},{56,40},{64,48},{72,56},{80,... | collective-permute-start | bytes 147464 | tf_op jit(solution)/shard_map/ppermute | solution.py:16
  68.6 41.9 %collective-permute-start.8 = (f32[64,192]{1,0:T(8,128)S(1)}, f32[64,192]{1,0:T(8,128)S(1)}, u32[]{:S(2)}, u32[]{:S(2)}) collective-permute-start(f32[64,192]{1,0:T(8,128)S(1)} %get-tuple-element.34), channel_id=1, source_target_pairs={{248,0},{0,8},{8,16},{16,24},{24,32},{32,40},{40,48},{48,56},{56,6... | collective-permute-start | bytes 147464 | tf_op jit(solution)/shard_map/ppermute | solution.py:16
  68.7 39.0 %collective-permute-start.15 = (f32[64,192]{1,0:T(8,128)S(1)}, f32[64,192]{1,0:T(8,128)S(1)}, u32[]{:S(2)}, u32[]{:S(2)}) collective-permute-start(f32[64,192]{1,0:T(8,128)S(1)} %get-tuple-element.35), channel_id=1, source_target_pairs={{32,0},{40,8},{48,16},{56,24},{64,32},{72,40},{80,48},{88,56},{96,... | collective-permute-start | bytes 147464 | tf_op jit(solution)/shard_map/ppermute | solution.py:16
  68.8 35.2 %collective-permute-start.14 = (f32[64,192]{1,0:T(8,128)S(1)}, f32[64,192]{1,0:T(8,128)}, u32[]{:S(2)}, u32[]{:S(2)}) collective-permute-start(f32[64,192]{1,0:T(8,128)S(1)} %get-tuple-element.36), channel_id=1, source_target_pairs={{224,0},{232,8},{240,16},{248,24},{0,32},{8,40},{16,48},{24,56},{3... | collective-permute-start | bytes 147464 | tf_op jit(solution)/shard_map/ppermute | solution.py:16
  71.9 28.5 %collective-permute-start.13 = (f32[64,192]{1,0:T(8,128)S(1)}, f32[64,192]{1,0:T(8,128)}, u32[]{:S(2)}, u32[]{:S(2)}) collective-permute-start(f32[64,192]{1,0:T(8,128)S(1)} %get-tuple-element.37), channel_id=1, source_target_pairs={{24,0},{32,8},{40,16},{48,24},{56,32},{64,40},{72,48},{80,56},{88,... | collective-permute-start | bytes 147464 | tf_op jit(solution)/shard_map/ppermute | solution.py:16
  73.5 23.3 %collective-permute-start.12 = (f32[64,192]{1,0:T(8,128)S(1)}, f32[64,192]{1,0:T(8,128)}, u32[]{:S(2)}, u32[]{:S(2)}) collective-permute-start(f32[64,192]{1,0:T(8,128)S(1)} %get-tuple-element.38), channel_id=1, source_target_pairs={{232,0},{240,8},{248,16},{0,24},{8,32},{16,40},{24,48},{32,56},{40... | collective-permute-start | bytes 147464 | tf_op jit(solution)/shard_map/ppermute | solution.py:16
  76.5 42.9 %all-to-all-start.1 = ((s32[8,48,1]{1,2,0:T(1,128)}), s32[8,48,1]{1,2,0:T(1,128)}, u32[]{:S(2)}, u32[]{:S(2)}) async-start(s32[8,48,1]{1,2,0:T(1,128)} %bitcast.177), calls=%async_computation.1 | async-start | bytes 8192 | tf_op jit(solution)/shard_map/all_to_all | solution.py:77
  119.4 9.9 %all-to-all-start = ((f32[8,1,3072]{2,1,0:T(1,128)}), f32[8,1,3072]{2,1,0:T(1,128)}, u32[]{:S(2)}, u32[]{:S(2)}) async-start(f32[8,1,3072]{2,1,0:T(1,128)} %reshape.680), calls=%async_computation | async-start | bytes 196608 | tf_op jit(solution)/shard_map/all_to_all | solution.py:106
  124.2 150.4 %all-reduce.4.cloned.1.call-start = ((), (), s32[]{:S(2)}) async-start(), calls=%async_computation.5 | async-start | bytes 524288 | tf_op jit(solution)/shard_map/psum | solution.py:110
  136.3 603.0 %all-reduce.6.cloned.1.call-start = ((), (), s32[]{:S(2)}) async-start(), calls=%async_computation.6 | async-start | bytes 524288 | tf_op jit(solution)/shard_map/psum | solution.py:110
  364.0 11.2 %collective-permute-start.19 = (f32[64,192]{1,0:T(8,128)S(1)}, f32[64,192]{1,0:T(8,128)}, u32[]{:S(2)}, u32[]{:S(2)}) collective-permute-start(f32[64,192]{1,0:T(8,128)S(1)} %get-tuple-element.31), channel_id=1, source_target_pairs={{16,0},{24,8},{32,16},{40,24},{48,32},{56,40},{64,48},{72,56},{80,... | collective-permute-start | bytes 147464 | tf_op jit(solution)/shard_map/ppermute | solution.py:16
  366.0 9.2 collective-permute-start.18
  367.0 10.9 %collective-permute-start.17 = (f32[64,192]{1,0:T(8,128)S(1)}, f32[64,192]{1,0:T(8,128)}, u32[]{:S(2)}, u32[]{:S(2)}) collective-permute-start(f32[64,192]{1,0:T(8,128)S(1)} %get-tuple-element.33), channel_id=1, source_target_pairs={{8,0},{16,8},{24,16},{32,24},{40,32},{48,40},{56,48},{64,56},{72,6... | collective-permute-start | bytes 147464 | tf_op jit(solution)/shard_map/ppermute | solution.py:16
  371.5 20.5 %collective-permute-start.20 = (f32[64,192]{1,0:T(8,128)}, f32[64,192]{1,0:T(8,128)}, u32[]{:S(2)}, u32[]{:S(2)}) collective-permute-start(f32[64,192]{1,0:T(8,128)} %get-tuple-element.30), channel_id=1, source_target_pairs={{232,0},{240,8},{248,16},{0,24},{8,32},{16,40},{24,48},{32,56},{40... | collective-permute-start | bytes 147464 | tf_op jit(solution)/shard_map/ppermute | solution.py:16
  371.7 22.1 %collective-permute-start.21 = (f32[64,192]{1,0:T(8,128)}, f32[64,192]{1,0:T(8,128)}, u32[]{:S(2)}, u32[]{:S(2)}) collective-permute-start(f32[64,192]{1,0:T(8,128)} %get-tuple-element.29), channel_id=1, source_target_pairs={{24,0},{32,8},{40,16},{48,24},{56,32},{64,40},{72,48},{80,56},{88,... | collective-permute-start | bytes 147464 | tf_op jit(solution)/shard_map/ppermute | solution.py:16
  375.2 20.4 %collective-permute-start.22 = (f32[64,192]{1,0:T(8,128)}, f32[64,192]{1,0:T(8,128)}, u32[]{:S(2)}, u32[]{:S(2)}) collective-permute-start(f32[64,192]{1,0:T(8,128)} %get-tuple-element.28), channel_id=1, source_target_pairs={{224,0},{232,8},{240,16},{248,24},{0,32},{8,40},{16,48},{24,56},{3... | collective-permute-start | bytes 147464 | tf_op jit(solution)/shard_map/ppermute | solution.py:16
  375.2 22.2 %collective-permute-start.23 = (f32[64,192]{1,0:T(8,128)}, f32[64,192]{1,0:T(8,128)}, u32[]{:S(2)}, u32[]{:S(2)}) collective-permute-start(f32[64,192]{1,0:T(8,128)} %get-tuple-element.27), channel_id=1, source_target_pairs={{32,0},{40,8},{48,16},{56,24},{64,32},{72,40},{80,48},{88,56},{96,... | collective-permute-start | bytes 147464 | tf_op jit(solution)/shard_map/ppermute | solution.py:16
  377.9 21.3 %collective-permute-start.16 = (f32[64,192]{1,0:T(8,128)}, f32[64,192]{1,0:T(8,128)}, u32[]{:S(2)}, u32[]{:S(2)}) collective-permute-start(f32[64,192]{1,0:T(8,128)} %get-tuple-element.26), channel_id=1, source_target_pairs={{248,0},{0,8},{8,16},{16,24},{24,32},{32,40},{40,48},{48,56},{56,6... | collective-permute-start | bytes 147464 | tf_op jit(solution)/shard_map/ppermute | solution.py:16
  489.4 9.1 collective-permute-start.27
  492.3 8.8 collective-permute-start.25
  494.9 8.7 collective-permute-start.29
  498.5 8.8 collective-permute-start.31
  812.0 11.0 %collective-permute-start.35 = (f32[64,192]{1,0:T(8,128)S(1)}, f32[64,192]{1,0:T(8,128)S(1)}, u32[]{:S(2)}, u32[]{:S(2)}) collective-permute-start(f32[64,192]{1,0:T(8,128)S(1)} %get-tuple-element.15), channel_id=1, source_target_pairs={{16,0},{24,8},{32,16},{40,24},{48,32},{56,40},{64,48},{72,56},{80,... | collective-permute-start | bytes 147464 | tf_op jit(solution)/shard_map/ppermute | solution.py:16
  813.9 9.1 collective-permute-start.34
  814.9 10.8 %collective-permute-start.33 = (f32[64,192]{1,0:T(8,128)S(1)}, f32[64,192]{1,0:T(8,128)S(1)}, u32[]{:S(2)}, u32[]{:S(2)}) collective-permute-start(f32[64,192]{1,0:T(8,128)S(1)} %get-tuple-element.17), channel_id=1, source_target_pairs={{8,0},{16,8},{24,16},{32,24},{40,32},{48,40},{56,48},{64,56},{72,6... | collective-permute-start | bytes 147464 | tf_op jit(solution)/shard_map/ppermute | solution.py:16
  819.4 10.3 %collective-permute-start.37 = (f32[64,192]{1,0:T(8,128)}, f32[64,192]{1,0:T(8,128)}, u32[]{:S(2)}, u32[]{:S(2)}) collective-permute-start(f32[64,192]{1,0:T(8,128)} %get-tuple-element.13), channel_id=1, source_target_pairs={{24,0},{32,8},{40,16},{48,24},{56,32},{64,40},{72,48},{80,56},{88,... | collective-permute-start | bytes 147464 | tf_op jit(solution)/shard_map/ppermute | solution.py:16
  823.0 10.3 %collective-permute-start.39 = (f32[64,192]{1,0:T(8,128)S(1)}, f32[64,192]{1,0:T(8,128)}, u32[]{:S(2)}, u32[]{:S(2)}) collective-permute-start(f32[64,192]{1,0:T(8,128)S(1)} %get-tuple-element.11), channel_id=1, source_target_pairs={{32,0},{40,8},{48,16},{56,24},{64,32},{72,40},{80,48},{88,56},{96,... | collective-permute-start | bytes 147464 | tf_op jit(solution)/shard_map/ppermute | solution.py:16
  825.7 9.5 %collective-permute-start.32 = (f32[64,192]{1,0:T(8,128)S(1)}, f32[64,192]{1,0:T(8,128)}, u32[]{:S(2)}, u32[]{:S(2)}) collective-permute-start(f32[64,192]{1,0:T(8,128)S(1)} %get-tuple-element.10), channel_id=1, source_target_pairs={{248,0},{0,8},{8,16},{16,24},{24,32},{32,40},{40,48},{48,56},{56,6... | collective-permute-start | bytes 147464 | tf_op jit(solution)/shard_map/ppermute | solution.py:16
  (68 other events, 2427.3 us)
Sparse Core Ops, SparseCore 0:
  136.4 138.1 all-reduce.3
  603.2 136.1 all-reduce.5
